TPU v7x, 256 devices: a whole 4x4x8 slice. The times are simulated.
256 devices in a mesh: dp: 4 (over y), space: 64 (over x, z, core).
Axes of the slice: x: 4, y: 4, z: 8, core: 2. Of those that a mesh axis runs over, the one named last changes fastest.
Arguments:
- volume: bfloat16 [4, 128, 4, 64, 128], P('dp', 'space'), may hold values from -30 to 30
- weights_one: bfloat16 [3, 3, 3, 128, 256], replicated, may hold values from -0.109375 to 0.109375
- gain_one: float32 [256], replicated, may hold values from 0.1 to 1.9
- shift_one: float32 [256], replicated, may hold values from -3 to 3
- weights_two: bfloat16 [3, 3, 3, 8, 256], P(None, None, None, None, 'space'), may hold values from -0.4375 to 0.4375
- gain_two: float32 [256], P('space'), may hold values from 0.1 to 1.9
- shift_two: float32 [256], P('space'), may hold values from -3 to 3
- upstream: bfloat16 [4, 256, 64, 2, 32], P('dp', 'space'), may hold values from -6 to 6
Outputs:
- result: bfloat16 [4, 256, 64, 2, 32], P('dp', 'space')
- grad_weights_one: float32 [3, 3, 3, 128, 256], P(None, None, None, None, 'space')
- grad_weights_two: float32 [3, 3, 3, 8, 256], P(None, None, None, None, 'space')
All inputs are finite; a program needn't handle non-finite values.
Results may differ from a plain program's by a relative error of at most 0.0057.
Values may be sent and summed in bfloat16 or wider, within the bound.
A program may use at most 64 MiB of HBM per device.

v0:
```python
import math
import jax
import jax.numpy as jnp
from jax import lax
from jax.sharding import PartitionSpec as P

EPS = 1e-05
LAST = ("NDHWC", "DHWIO", "NDHWC")
FIRST = ("NCDHW", "DHWIO", "NCDHW")


def from_behind(value, axis, steps):
    count = lax.axis_size(axis)
    leading, last = (max(0, -steps), min(count, count - steps))
    return lax.ppermute(value, axis, [(source, source + steps) for source in range(leading, last)])


def combined_all(part, axis, combine):
    gathered = jax.tree.map(lambda a: lax.all_gather(a, axis), part)

    def take(source):
        return jax.tree.map(lambda a: lax.dynamic_index_in_dim(a, source, 0, False), gathered)

    return lax.fori_loop(
        1, lax.axis_size(axis), lambda source, state: combine(state, take(source)), take(0)
    )


def welford(left, right):
    count_a, mean_a, spread_a = left
    count_b, mean_b, spread_b = right
    merged = count_a + count_b
    delta = mean_b - mean_a
    return (
        merged,
        mean_a + delta * (count_b / merged),
        spread_a + spread_b + delta * delta * (count_a * count_b / merged),
    )


def group_filter(inputs, grads):
    return lax.conv_general_dilated(
        inputs,
        grads,
        (1, 1, 1),
        ((1, 1), (1, 1), (1, 1)),
        dimension_numbers=("CNDHW", "IODHW", "DHWNC"),
        preferred_element_type=jnp.float32,
    )


def per_device(
    volume, weights_one, gain_one, shift_one, weights_two, gain_two, shift_two, upstream
):
    planes = lax.axis_size("space")
    below = from_behind(volume[:, 1:], "space", 1)
    stacked = jnp.concatenate([below, volume], axis=1)
    pre_one = lax.conv_general_dilated(
        stacked,
        weights_one,
        (2, 2, 2),
        ((0, 0), (1, 1), (1, 1)),
        dimension_numbers=LAST,
        preferred_element_type=jnp.float32,
    )
    lead = pre_one.shape[0]
    count = float(lax.axis_size("dp") * lead * planes * pre_one.shape[2] * pre_one.shape[3])
    axes_last = (0, 1, 2, 3)
    mean_one = lax.psum(jnp.sum(pre_one, axis=axes_last), ("dp", "space")) / count
    spread_one = lax.psum(jnp.sum(jnp.square(pre_one - mean_one), axis=axes_last), ("dp", "space"))
    var_one = spread_one / count
    inv_one = lax.rsqrt(var_one + EPS)
    norm_one = (pre_one - mean_one) * inv_one
    act_in = norm_one * gain_one + shift_one
    activated = jax.nn.silu(act_in).astype(jnp.bfloat16)
    act_first = jnp.transpose(activated, (0, 4, 1, 2, 3))
    own_width = weights_two.shape[4]
    group_width = weights_two.shape[3]
    window = max(own_width, group_width)
    replicas = window // own_width
    channels = act_first.shape[1]
    tail = act_first.shape[2:]
    parts = act_first.reshape((lead, channels // window, 1, window) + tail)
    copies = jnp.broadcast_to(parts, (lead, channels // window, replicas, window) + tail)
    outgoing = copies.reshape((lead, planes * window) + tail)
    inputs = lax.all_to_all(outgoing, "space", split_axis=1, concat_axis=2, tiled=True)
    groups_here = window // group_width
    per_group = own_width // groups_here
    padding_one = ((1, 1), (1, 1), (1, 1))
    pre_two = lax.conv_general_dilated(
        inputs,
        weights_two,
        (1, 1, 1),
        padding_one,
        dimension_numbers=FIRST,
        feature_group_count=groups_here,
        preferred_element_type=jnp.float32,
    )
    axes_first = (0, 2, 3, 4)
    local_mean_two = jnp.mean(pre_two, axis=axes_first, keepdims=True)
    local_spread_two = jnp.sum(jnp.square(pre_two - local_mean_two), axis=axes_first, keepdims=True)
    local_count_two = float(pre_two.size // pre_two.shape[1])
    merged_two, mean_two, spread_two = combined_all(
        (jnp.full((1, 1, 1, 1, 1), local_count_two, jnp.float32), local_mean_two, local_spread_two),
        "dp",
        welford,
    )
    inv_two = lax.rsqrt(spread_two / merged_two + EPS)
    norm_two = (pre_two - mean_two) * inv_two
    gain_col = gain_two.reshape((1, -1, 1, 1, 1))
    shift_col = shift_two.reshape((1, -1, 1, 1, 1))
    result = (norm_two * gain_col + shift_col).astype(jnp.bfloat16)
    grad_norm_two = upstream.astype(jnp.float32) * gain_col * (1.0 / math.sqrt(count))
    first_sum, second_sum = lax.psum(
        (
            jnp.sum(grad_norm_two, axis=axes_first, keepdims=True),
            jnp.sum(grad_norm_two * norm_two, axis=axes_first, keepdims=True),
        ),
        "dp",
    )
    grad_pre_two = (
        inv_two * (grad_norm_two - first_sum / count - norm_two * (second_sum / count))
    ).astype(jnp.bfloat16)
    grouped_inputs = inputs.reshape((lead, groups_here, group_width) + inputs.shape[2:])
    grouped_grads = grad_pre_two.reshape((lead, groups_here, per_group) + grad_pre_two.shape[2:])
    pieces = jax.vmap(group_filter, in_axes=(1, 1))(grouped_inputs, grouped_grads)
    local_two = jnp.transpose(pieces, (1, 2, 3, 4, 0, 5)).reshape((3, 3, 3, group_width, own_width))
    grad_weights_two = lax.psum(local_two, "dp")
    flipped = weights_two[::-1, ::-1, ::-1]
    turned = (
        flipped.reshape((3, 3, 3, group_width, groups_here, per_group))
        .transpose((0, 1, 2, 5, 4, 3))
        .reshape((3, 3, 3, per_group, window))
    )
    partial_grad = lax.conv_general_dilated(
        grad_pre_two,
        turned,
        (1, 1, 1),
        padding_one,
        dimension_numbers=FIRST,
        feature_group_count=groups_here,
        preferred_element_type=jnp.float32,
    )
    arrived = lax.all_to_all(partial_grad, "space", split_axis=2, concat_axis=1, tiled=True)
    grad_act = jnp.sum(
        arrived.reshape((lead, channels // window, replicas, window) + arrived.shape[2:]), axis=2
    ).reshape((lead, channels) + arrived.shape[2:])
    grad_last = jnp.transpose(grad_act, (0, 2, 3, 4, 1))
    sigma = jax.nn.sigmoid(act_in)
    grad_norm_one = grad_last * (sigma * (1.0 + act_in * (1.0 - sigma))) * gain_one
    third_sum, fourth_sum = lax.psum(
        (jnp.sum(grad_norm_one, axis=axes_last), jnp.sum(grad_norm_one * norm_one, axis=axes_last)),
        ("dp", "space"),
    )
    grad_pre_one = (
        inv_one * (grad_norm_one - third_sum / count - norm_one * (fourth_sum / count))
    ).astype(jnp.bfloat16)
    local_one = lax.conv_general_dilated(
        stacked,
        grad_pre_one,
        (1, 1, 1),
        ((0, 0), (1, 0), (1, 0)),
        rhs_dilation=(2, 2, 2),
        dimension_numbers=("CDHWN", "IDHWO", "DHWNC"),
        preferred_element_type=jnp.float32,
    )
    summed = lax.psum(local_one, "dp")
    grad_weights_one = lax.psum_scatter(summed, "space", scatter_dimension=4, tiled=True)
    return (result, grad_weights_one, grad_weights_two)


def solution(mesh):
    return jax.shard_map(
        per_device,
        mesh=mesh,
        in_specs=(
            P("dp", "space", None, None, None),
            P(),
            P(),
            P(),
            P(None, None, None, None, "space"),
            P("space"),
            P("space"),
            P("dp", "space", None, None, None),
        ),
        out_specs=(
            P("dp", "space", None, None, None),
            P(None, None, None, None, "space"),
            P(None, None, None, None, "space"),
        ),
        check_vma=False,
    )
```

profile of v0, /device:TPU:2, one launch (start us, length us, event | category | flops | bytes accessed | tf_op | source)
XLA Modules:
  0.0 559.2 jit_solution(1003987523249396105)
XLA Ops:
  7.2 1.0 slice.21
  8.3 1.9 collective-permute-start
  10.2 7.9 %collective-permute-done = bf16[1,1,4,64,128]{4,0,3,2,1:T(2,128)(2,1)S(1)} collective-permute-done((bf16[1,1,4,64,128]{4,0,3,2,1:T(2,128)(2,1)S(1)}, bf16[1,1,4,64,128]{4,0,3,2,1:T(2,128)(2,1)S(1)}, u32[]{:S(2)}, u32[]{:S(2)}) %collective-permute-start) | collective-permute-done | bytes 65568 | tf_op jit(solution)/shard_map/ppermute | solution.py:15
  18.2 1.1 constant_dynamic-update-slice_fusion
  19.4 0.7 copy-done.1
  21.0 74.9 %psum.56 = f32[256]{0:T(256)S(1)} all-reduce(f32[256]{0:T(256)S(1)} %get-tuple-element.289), channel_id=1, replica_groups=mesh['dp'=4,'space'=64] {'dp','space'}, use_global_device_ids=true, to_apply=%region_1.0 | all-reduce | flops 256 | bytes 2048 | tf_op jit(solution)/shard_map/psum | solution.py:69
  95.9 74.4 %psum.57 = f32[256]{0:T(256)S(1)} all-reduce(f32[256]{0:T(256)S(1)} %select_reduce_fusion.2), channel_id=1, replica_groups=mesh['dp'=4,'space'=64] {'dp','space'}, use_global_device_ids=true, to_apply=%region_3.0 | all-reduce | flops 256 | bytes 2048 | tf_op jit(solution)/shard_map/psum | solution.py:70
  170.5 0.4 copy-done.9
  171.3 0.8 reshape.180
  172.2 8.1 %all-to-all-start = ((bf16[64,2,256]{2,1,0:T(2,128)(2,1)}), bf16[64,2,256]{2,1,0:T(2,128)(2,1)S(1)}, u32[]{:S(2)}, u32[]{:S(2)}) async-start(bf16[64,2,256]{2,1,0:T(2,128)(2,1)} %reshape.180), calls=%async_computation | async-start | bytes 131072 | tf_op jit(solution)/shard_map/all_to_all | solution.py:86
  180.3 0.6 rev.3
  180.9 0.6 dynamic-slice
  182.2 0.8 dynamic-update-slice
  183.0 6.0 %all-to-all-done = bf16[64,2,256]{2,1,0:T(2,128)(2,1)S(1)} async-done(((bf16[64,2,256]{2,1,0:T(2,128)(2,1)}), bf16[64,2,256]{2,1,0:T(2,128)(2,1)S(1)}, u32[]{:S(2)}, u32[]{:S(2)}) %all-to-all-start) | async-done | bytes 65568 | tf_op jit(solution)/shard_map/all_to_all | solution.py:86
  189.5 0.7 pad.2.clone
  190.2 2.1 copy.207
  192.5 5.6 fusion.8
  198.1 1.7 copy.208
  200.5 8.6 %all-reduce.7 = (f32[4]{0:T(128)S(1)}, f32[16]{0:T(128)S(1)}, f32[16]{0:T(128)S(1)}) all-reduce(f32[4]{0:T(128)S(1)} %dynamic-update-slice, f32[16]{0:T(128)S(1)} %get-tuple-element.288, f32[16]{0:T(128)S(1)} %dynamic-update-slice.2), channel_id=1, replica_groups=mesh['dp'=4,'space'=64] {'dp'}, use_global_device_ids=true, to_apply=%add | all-reduce | flops 36 | bytes 288
  209.8 13.6 %while.19 = (s32[]{:T(128)}, f32[1,1,1,1,1]{4,3,2,1,0:T(1,128)}, f32[1,4,1,1,1]{1,4,3,2,0:T(1,128)S(1)}, f32[1,4,1,1,1]{1,4,3,2,0:T(1,128)S(1)}, f32[4,1,1,1,1,1...) while((s32[]{:T(128)}, f32[1,1,1,1,1]{4,3,2,1,0:T(1,128)}, ...), condition=%wide.region_7.8_spmd, body=%wide.region_6.7_spmd.sunk | while | flops 37 | bytes 303 | solution.py:24
  209.8 0.6 constant_dynamic-slice_fusion.5
  214.4 0.6 constant_dynamic-slice_fusion.5
  218.9 0.6 constant_dynamic-slice_fusion.5
  223.5 0.7 rsqrt_bitcast_fusion
  224.1 0.8 add_convert_fusion
  225.2 9.4 %all-reduce.6 = (f32[1,4,1,1,1]{1,4,3,2,0:T(1,128)S(1)}, f32[1,4,1,1,1]{1,4,3,2,0:T(1,128)S(1)}) all-reduce(f32[1,4,1,1,1]{1,4,3,2,0:T(1,128)S(1)} %bitcast.177, f32[1,4,1,1,1]{1,4,3,2,0:T(1,128)S(1)} %bitcast.176), channel_id=1, replica_groups=mesh['dp'=4,'space'=64] {'dp'}, use_global_device_ids=true, to_apply=%region_11.12 | all-reduce | flops 8 | bytes 64 | tf_op jit(solution)/shard_map/psum | solution.py:114
  235.5 6.9 %convolution_select_fusion = f32[64,2,8,5,8]{4,2,3,1,0:T(8,128)} fusion(pred[8,5]{0,1:T(8,128)(4,1)S(1)} %copy-done.7, bf16[4,64,2,1,7,2]{4,0,5,2,1,3:T(4,128)(2,1)S(1)} %slice.28, bf16[4,64,2,1,8,5]{4,0,5,2,1,3:T(4,128)(2,1)S(1)} %copy.218, bf16[3,3,3,8,4]{3,4,2,1,0:T(4,128)(2,1)S(1)} %copy-done.6), kind=kOutput, calls=%fused_computation.19 | convolution fusion | flops 6049792 | bytes 220904 | tf_op jit(solution)/shard_map/conv_general_dilated | solution.py:135
  242.5 2.6 copy.219
  245.4 0.9 reshape.182
  246.4 5.5 all-to-all-start.1
  252.2 0.8 copy.241
  253.0 8.2 %all-to-all-done.1 = f32[64,1,512]{2,1,0:T(1,128)S(1)} async-done(((f32[64,1,512]{2,1,0:T(1,128)}), f32[64,1,512]{2,1,0:T(1,128)S(1)}, u32[]{:S(2)}, u32[]{:S(2)}) %all-to-all-start.1) | async-done | bytes 131104 | tf_op jit(solution)/shard_map/all_to_all | solution.py:144
  261.2 0.5 broadcast.186
  261.7 0.9 reduce.1
  262.9 0.7 reduce_sum.87
  263.6 1.3 fusion.51
  264.9 73.3 %all-reduce.4 = (f32[256]{0:T(256)S(1)}, f32[256]{0:T(256)S(1)}) all-reduce(f32[256]{0:T(256)S(1)} %get-tuple-element.252, f32[256]{0:T(256)S(1)} %get-tuple-element.251), channel_id=1, replica_groups=mesh['dp'=4,'space'=64] {'dp','space'}, use_global_device_ids=true, to_apply=%region_16.17 | all-reduce | flops 512 | bytes 4096 | tf_op jit(solution)/shard_map/psum | solution.py:151
  338.4 0.8 fusion.31
  339.4 2.8 fusion.53
  342.3 0.6 copy-done.13
  342.9 0.6 dynamic-slice.3
  344.1 3.5 copy.231
  347.7 0.6 copy.232
  348.3 3.4 copy.230
  351.7 29.6 %fusion.54 = f32[3,3,3,8,4]{3,4,2,1,0:T(4,128)S(1)} fusion(bf16[1,8,64,2,32]{1,0,4,3,2:T(2,128)(2,1)} %copy.230, bf16[1,4,64,2,32]{1,0,4,3,2:T(2,128)(2,1)} %copy.231), kind=kOutput, calls=%fused_computation.97 | convolution fusion | flops 4572160 | bytes 101760 | tf_op jit(solution)/shard_map/vmap()/conv_general_dilated | solution.py:42
  381.3 151.0 %all-reduce.10.cloned.1.call-done = f32[3,3,3,128,256]{3,4,2,1,0:T(8,128)} async-done(((f32[3,3,3,128,256]{3,4,2,1,0:T(8,128)}), f32[3,3,3,128,256]{3,4,2,1,0:T(8,128)}) %all-reduce.10.cloned.1.call-update) | async-done | bytes 3538960
  532.3 0.9 constant_dynamic-slice_fusion.3
  533.3 18.7 %all-reduce.5 = (f32[3,3,3,128,4]{3,4,2,1,0:T(4,128)}, f32[3,3,3,8,4]{3,4,2,1,0:T(4,128)}) all-reduce(f32[3,3,3,128,4]{3,4,2,1,0:T(4,128)S(1)} %constant_dynamic-slice_fusion.3, f32[3,3,3,8,4]{3,4,2,1,0:T(4,128)S(1)} %fusion.54), channel_id=1, replica_groups=mesh['dp'=4,'space'=64] {'dp'}, use_global_device_ids=true, to_apply=%region_17.18 | all-reduce | flops 14688 | bytes 117504 | tf_op jit(solution)/shard_map/psum | solution.py:167
  (91 shorter events, 5.7 us)
Async XLA Ops:
  7.2 13.3 %copy-start = (bf16[3,3,3,128,256]{4,3,2,1,0:T(8,128)(2,1)S(1)}, bf16[3,3,3,128,256]{4,3,2,1,0:T(8,128)(2,1)}, u32[]{:S(2)}) copy-start(bf16[3,3,3,128,256]{4,3,2,1,0:T(8,128)(2,1)} %param.11) | copy-start | bytes 5308420
  7.2 13.3 %copy-start.7 = (pred[8,5]{0,1:T(8,128)(4,1)S(1)}, pred[8,5]{0,1:T(8,128)(4,1)}, u32[]{:S(2)}) copy-start(pred[8,5]{0,1:T(8,128)(4,1)} %constant.99) | copy-start | bytes 124
  8.3 9.8 %collective-permute-start = (bf16[1,1,4,64,128]{4,0,3,2,1:T(2,128)(2,1)S(1)}, bf16[1,1,4,64,128]{4,0,3,2,1:T(2,128)(2,1)S(1)}, u32[]{:S(2)}, u32[]{:S(2)}) collective-permute-start(bf16[1,1,4,64,128]{4,0,3,2,1:T(2,128)(2,1)S(1)} %copy.254), channel_id=1, source_target_pairs={{0,1},{1,2},{2,3},{3,4},{4,5},{5,6},{6,7},{7,8},{8,9},{9,10},{10,1... | collective-permute-start | bytes 196616 | tf_op jit(solution)/shard_map/ppermute | solution.py:15
  19.4 0.7 copy-start.1
  20.1 150.2 %copy-start.8 = (f32[256]{0:T(256)S(1)}, f32[256]{0:T(256)}, u32[]{:S(2)}) copy-start(f32[256]{0:T(256)} %param.12) | copy-start | bytes 3076
  20.1 150.2 %copy-start.11 = (f32[256]{0:T(256)S(1)}, f32[256]{0:T(256)}, u32[]{:S(2)}) copy-start(f32[256]{0:T(256)} %param.13) | copy-start | bytes 3076
  20.5 159.8 %copy-start.5 = (bf16[3,3,3,8,4]{3,4,2,1,0:T(4,128)(2,1)S(1)}, bf16[3,3,3,8,4]{3,4,2,1,0:T(4,128)(2,1)}, u32[]{:S(2)}) copy-start(bf16[3,3,3,8,4]{3,4,2,1,0:T(4,128)(2,1)} %param.14) | copy-start | bytes 5188
  20.5 160.4 %copy-start.14 = (u32[256]{0:T(256)S(1)}, u32[256]{0:T(256)}, u32[]{:S(2)}) copy-start(u32[256]{0:T(256)} %constant.108) | copy-start | bytes 3076
  170.3 0.6 copy-start.9
  172.2 16.9 %all-to-all-start = ((bf16[64,2,256]{2,1,0:T(2,128)(2,1)}), bf16[64,2,256]{2,1,0:T(2,128)(2,1)S(1)}, u32[]{:S(2)}, u32[]{:S(2)}) async-start(bf16[64,2,256]{2,1,0:T(2,128)(2,1)} %reshape.180), calls=%async_computation | async-start | bytes 131072 | tf_op jit(solution)/shard_map/all_to_all | solution.py:86
  198.1 26.0 %copy-start.10 = (f32[4]{0:T(128)S(1)}, f32[4]{0:T(128)}, u32[]{:S(2)}) copy-start(f32[4]{0:T(128)} %param.15) | copy-start | bytes 52
  198.1 26.1 %copy-start.12 = (f32[4]{0:T(128)S(1)}, f32[4]{0:T(128)}, u32[]{:S(2)}) copy-start(f32[4]{0:T(128)} %param.16) | copy-start | bytes 52
  198.1 26.9 %copy-start.4 = (bf16[1,4,64,2,32]{2,4,3,1,0:T(8,128)(2,1)S(1)}, bf16[1,4,64,2,32]{2,4,3,1,0:T(8,128)(2,1)}, u32[]{:S(2)}) copy-start(bf16[1,4,64,2,32]{2,4,3,1,0:T(8,128)(2,1)} %param.17) | copy-start | bytes 98308
  199.8 35.7 %copy-start.6 = (bf16[3,3,3,8,4]{3,4,2,1,0:T(4,128)(2,1)S(1)}, bf16[3,3,3,8,4]{3,4,2,1,0:T(4,128)(2,1)}, u32[]{:S(2)}) copy-start(bf16[3,3,3,8,4]{3,4,2,1,0:T(4,128)(2,1)} %rev.3) | copy-start | bytes 5188
  246.4 14.9 %all-to-all-start.1 = ((f32[64,1,512]{2,1,0:T(1,128)}), f32[64,1,512]{2,1,0:T(1,128)S(1)}, u32[]{:S(2)}, u32[]{:S(2)}) async-start(f32[64,1,512]{2,1,0:T(1,128)} %reshape.182), calls=%async_computation.1 | async-start | bytes 262144 | tf_op jit(solution)/shard_map/all_to_all | solution.py:144
  251.8 280.5 %all-reduce.10.cloned.1.call-start = ((), (), s32[]{:S(2)}) async-start(), calls=%async_computation.2 | async-start | bytes 7077888
  262.7 76.7 %copy-start.2 = (bf16[1,3,4,64,128]{4,0,3,2,1:T(2,128)(2,1)S(1)}, bf16[1,3,4,64,128]{4,0,3,2,1:T(2,128)(2,1)}, u32[]{:S(2)}) copy-start(bf16[1,3,4,64,128]{4,0,3,2,1:T(2,128)(2,1)} %copy-done.1) | copy-start | bytes 589828
  342.2 0.7 copy-start.13
  342.2 5.4 copy-start.3
Sparse Core Ops, SparseCore 0:
  342.4 189.9 all-reduce.9
where the time goes:
time: 568 us; the launch traced here: 559 us
  blocking collectives  259 us (46%)
  waiting for transfers between devices  173 us (30%)
  matrix products  45.4 us (8%)
  local copies, waits for them, and re-layouts  31 us (5%)
  between operations  16.8 us (3%)
  starting transfers between devices  15.5 us (3%)
  loops' own time  11.6 us (2%)
  other arithmetic  6.47 us (1%)
    unnamed x2, waiting for transfers between devices  151 us
    psum x1, blocking collectives, per_device(): lax.psum(jnp.sum(pre_one, axis=axes_last), ('dp', 'space')) / count  74.9 us
    psum x1, blocking collectives, per_device(): lax.psum(jnp.sum(jnp.square(pre_one - mean_one), axis=axes_last), ('dp',...  74.4 us
    psum x1, blocking collectives, per_device(): lax.psum((jnp.sum(grad_norm_one, axis=axes_last), jnp.sum(grad_norm_one *...  73.3 us
    conv_general_dilated x1, matrix products, group_filter(): lax.conv_general_dilated(inputs, grads, (1, 1, 1), ((1, 1), (1, 1), (1, 1...  29.6 us
    psum x1, blocking collectives, per_device(): summed = lax.psum(local_one, 'dp')  18.7 us
    another operation x1, loops' own time, combined_all(): lax.fori_loop(1, lax.axis_size(axis), lambda source, state: combine(state...  11.6 us
  transfers between devices with their start and end apart: 4, of which 4 were waited for; matrix products, arithmetic and copies ran while one was open for 7% of the time, Pallas kernels for 0%

commit v1 on v0

--- a/solution.py
+++ b/solution.py
@@ -141,7 +141,12 @@
         feature_group_count=groups_here,
         preferred_element_type=jnp.float32,
     )
-    arrived = lax.all_to_all(partial_grad, "space", split_axis=2, concat_axis=1, tiled=True)
+    arrived = jnp.concatenate(
+        lax.all_to_all(
+            jnp.stack(jnp.split(partial_grad, lax.axis_size("space"), axis=2)), "space", 0, 0
+        ),
+        axis=1,
+    )
     grad_act = jnp.sum(
         arrived.reshape((lead, channels // window, replicas, window) + arrived.shape[2:]), axis=2
     ).reshape((lead, channels) + arrived.shape[2:])

time: 568 us -> 665 us (1.17)
  local copies, waits for them, and re-layouts: 31 us -> 125 us
    conv_general_dilated x5 -> x134, local copies, waits for them, and re-layouts: 3.54 us -> 78.9 us  [per_device(): lax.conv_general_dilated(grad_pre_two, turned, (1, 1, 1), padding_one, di...]
    unnamed x51 -> x198, local copies, waits for them, and re-layouts: 9.49 us -> 28.3 us
  transfers between devices with their start and end apart: 4 -> 4, of which waited for: 4 -> 4; matrix products, arithmetic and copies ran while one was open for 7% -> 6% of each run, Pallas kernels for 0% -> 0%
where the time goes in v1:
time: 665 us; the launch traced here: 653 us
  blocking collectives  259 us (39%)
  waiting for transfers between devices  174 us (26%)
  local copies, waits for them, and re-layouts  125 us (19%)
  matrix products  43.9 us (7%)
  between operations  17.7 us (3%)
  starting transfers between devices  15.5 us (2%)
  loops' own time  11.3 us (2%)
  other arithmetic  6.98 us (1%)
    unnamed x2, waiting for transfers between devices  151 us
    conv_general_dilated x134, local copies, waits for them, and re-layouts, per_device(): lax.conv_general_dilated(grad_pre_two, turned, (1, 1, 1), padding_one, di...  78.9 us
    psum x1, blocking collectives, per_device(): lax.psum(jnp.sum(pre_one, axis=axes_last), ('dp', 'space')) / count  74.9 us
    psum x1, blocking collectives, per_device(): lax.psum(jnp.sum(jnp.square(pre_one - mean_one), axis=axes_last), ('dp',...  74.4 us
    psum x1, blocking collectives, per_device(): lax.psum((jnp.sum(grad_norm_one, axis=axes_last), jnp.sum(grad_norm_one *...  73.3 us
    conv_general_dilated x1, matrix products, group_filter(): lax.conv_general_dilated(inputs, grads, (1, 1, 1), ((1, 1), (1, 1), (1, 1...  29.6 us
    unnamed x198, local copies, waits for them, and re-layouts  28.3 us
    psum x1, blocking collectives, per_device(): summed = lax.psum(local_one, 'dp')  18.7 us
  transfers between devices with their start and end apart: 4, of which 4 were waited for; matrix products, arithmetic and copies ran while one was open for 6% of the time, Pallas kernels for 0%

profile of v1, /device:TPU:2, one launch (start us, length us, event | category | flops | bytes accessed | tf_op | source)
XLA Modules:
  0.0 653.4 jit_solution(11982604458277611306)
XLA Ops:
  7.2 1.0 slice.148
  8.3 1.9 collective-permute-start
  10.2 7.9 %collective-permute-done = bf16[1,1,4,64,128]{4,0,3,2,1:T(2,128)(2,1)S(1)} collective-permute-done((bf16[1,1,4,64,128]{4,0,3,2,1:T(2,128)(2,1)S(1)}, bf16[1,1,4,64,128]{4,0,3,2,1:T(2,128)(2,1)S(1)}, u32[]{:S(2)}, u32[]{:S(2)}) %collective-permute-start) | collective-permute-done | bytes 65568 | tf_op jit(solution)/shard_map/ppermute | solution.py:15
  18.2 1.1 constant_dynamic-update-slice_fusion
  21.0 74.9 %psum.56 = f32[256]{0:T(256)S(1)} all-reduce(f32[256]{0:T(256)S(1)} %get-tuple-element.333), channel_id=1, replica_groups=mesh['dp'=4,'space'=64] {'dp','space'}, use_global_device_ids=true, to_apply=%region_1.0 | all-reduce | flops 256 | bytes 2048 | tf_op jit(solution)/shard_map/psum | solution.py:69
  96.0 74.4 %psum.57 = f32[256]{0:T(256)S(1)} all-reduce(f32[256]{0:T(256)S(1)} %select_reduce_fusion.2), channel_id=1, replica_groups=mesh['dp'=4,'space'=64] {'dp','space'}, use_global_device_ids=true, to_apply=%region_3.0 | all-reduce | flops 256 | bytes 2048 | tf_op jit(solution)/shard_map/psum | solution.py:70
  172.0 8.1 %all-to-all-start = ((bf16[64,2,256]{2,1,0:T(2,128)(2,1)}), bf16[64,2,256]{2,1,0:T(2,128)(2,1)S(1)}, u32[]{:S(2)}, u32[]{:S(2)}) async-start(bf16[64,2,256]{2,1,0:T(2,128)(2,1)} %reshape.364), calls=%async_computation | async-start | bytes 131072 | tf_op jit(solution)/shard_map/all_to_all | solution.py:86
  182.7 6.1 all-to-all-done
  190.0 2.1 copy.511
  192.3 5.6 fusion.8
  197.9 1.7 copy.512
  200.4 8.6 %all-reduce.7 = (f32[4]{0:T(128)S(1)}, f32[16]{0:T(128)S(1)}, f32[16]{0:T(128)S(1)}) all-reduce(f32[4]{0:T(128)S(1)} %dynamic-update-slice, f32[16]{0:T(128)S(1)} %get-tuple-element.332, f32[16]{0:T(128)S(1)} %dynamic-update-slice.2), channel_id=1, replica_groups=mesh['dp'=4,'space'=64] {'dp'}, use_global_device_ids=true, to_apply=%add | all-reduce | flops 36 | bytes 288
  209.6 13.3 %while.19 = (s32[]{:T(128)}, f32[1,1,1,1,1]{4,3,2,1,0:T(1,128)}, f32[1,4,1,1,1]{1,4,3,2,0:T(1,128)S(1)}, f32[1,4,1,1,1]{1,4,3,2,0:T(1,128)S(1)}, f32[4,1,1,1,1,1...) while((s32[]{:T(128)}, f32[1,1,1,1,1]{4,3,2,1,0:T(1,128)}, ...), condition=%wide.region_7.8_spmd, body=%wide.region_6.7_spmd.sunk | while | flops 37 | bytes 303 | solution.py:24
  224.7 9.1 %all-reduce.6 = (f32[1,4,1,1,1]{1,4,3,2,0:T(1,128)S(1)}, f32[1,4,1,1,1]{1,4,3,2,0:T(1,128)S(1)}) all-reduce(f32[1,4,1,1,1]{1,4,3,2,0:T(1,128)S(1)} %bitcast.935, f32[1,4,1,1,1]{1,4,3,2,0:T(1,128)S(1)} %bitcast.934), channel_id=1, replica_groups=mesh['dp'=4,'space'=64] {'dp'}, use_global_device_ids=true, to_apply=%region_11.12 | all-reduce | flops 8 | bytes 64 | tf_op jit(solution)/shard_map/psum | solution.py:114
  235.4 5.5 convolution_select_fusion
  248.8 1.0 copy.572
  250.4 0.9 copy.570
  252.0 0.9 copy.568
  253.6 0.9 copy.566
  255.3 0.9 copy.564
  256.9 0.9 copy.562
  258.5 0.9 copy.560
  260.1 0.9 copy.558
  261.8 0.9 copy.556
  266.6 0.9 copy.550
  276.4 0.9 copy.538
  280.6 1.0 copy.610
  283.3 1.0 copy.644
  284.3 1.0 copy.642
  285.4 1.0 copy.640
  287.0 0.9 copy.638
  288.6 0.9 copy.636
  291.9 0.9 copy.632
  295.1 0.9 copy.628
  301.6 0.9 copy.620
  326.6 12.5 %reshape.366 = f32[64,1,512]{2,1,0:T(1,128)} reshape(f32[64,1,1,2,8,32]{5,4,3,2,1,0:T(8,128)S(1)} %bitcast.858) | data formatting | bytes 262144
  339.2 5.5 all-to-all-start.1
  345.1 8.9 %all-to-all-done.1 = f32[64,1,512]{2,1,0:T(1,128)S(1)} async-done(((f32[64,1,512]{2,1,0:T(1,128)}), f32[64,1,512]{2,1,0:T(1,128)S(1)}, u32[]{:S(2)}, u32[]{:S(2)}) %all-to-all-start.1) | async-done | bytes 131104 | tf_op jit(solution)/shard_map/all_to_all | solution.py:145
  354.6 1.6 reduce.1
  356.2 1.1 reshape.367
  358.1 1.2 fusion.51
  359.3 73.3 %all-reduce.4 = (f32[256]{0:T(256)S(1)}, f32[256]{0:T(256)S(1)}) all-reduce(f32[256]{0:T(256)S(1)} %get-tuple-element.232, f32[256]{0:T(256)S(1)} %get-tuple-element.231), channel_id=1, replica_groups=mesh['dp'=4,'space'=64] {'dp','space'}, use_global_device_ids=true, to_apply=%region_16.17 | all-reduce | flops 512 | bytes 4096 | tf_op jit(solution)/shard_map/psum | solution.py:156
  433.7 2.8 fusion.57
  438.4 3.5 copy.660
  442.6 3.2 copy.659
  445.8 29.6 %fusion.58 = f32[3,3,3,8,4]{3,4,2,1,0:T(4,128)S(1)} fusion(bf16[1,8,64,2,32]{1,0,4,3,2:T(2,128)(2,1)} %copy.659, bf16[1,4,64,2,32]{1,0,4,3,2:T(2,128)(2,1)} %copy.660), kind=kOutput, calls=%fused_computation.228 | convolution fusion | flops 4572160 | bytes 101760 | tf_op jit(solution)/shard_map/vmap()/conv_general_dilated | solution.py:42
  475.4 151.1 %all-reduce.10.cloned.1.call-done = f32[3,3,3,128,256]{3,4,2,1,0:T(8,128)} async-done(((f32[3,3,3,128,256]{3,4,2,1,0:T(8,128)}), f32[3,3,3,128,256]{3,4,2,1,0:T(8,128)}) %all-reduce.10.cloned.1.call-update) | async-done | bytes 3538960
  627.5 18.7 %all-reduce.5 = (f32[3,3,3,128,4]{3,4,2,1,0:T(4,128)}, f32[3,3,3,8,4]{3,4,2,1,0:T(4,128)}) all-reduce(f32[3,3,3,128,4]{3,4,2,1,0:T(4,128)S(1)} %constant_dynamic-slice_fusion.3, f32[3,3,3,8,4]{3,4,2,1,0:T(4,128)S(1)} %fusion.58), channel_id=1, replica_groups=mesh['dp'=4,'space'=64] {'dp'}, use_global_device_ids=true, to_apply=%region_17.18 | all-reduce | flops 14688 | bytes 117504 | tf_op jit(solution)/shard_map/psum | solution.py:172
  (368 shorter events, 84.4 us)
Async XLA Ops:
  7.2 13.3 %copy-start = (bf16[3,3,3,128,256]{4,3,2,1,0:T(8,128)(2,1)S(1)}, bf16[3,3,3,128,256]{4,3,2,1,0:T(8,128)(2,1)}, u32[]{:S(2)}) copy-start(bf16[3,3,3,128,256]{4,3,2,1,0:T(8,128)(2,1)} %param.11) | copy-start | bytes 5308420
  7.2 13.3 %copy-start.49 = (pred[8,5]{0,1:T(8,128)(4,1)S(1)}, pred[8,5]{0,1:T(8,128)(4,1)}, u32[]{:S(2)}) copy-start(pred[8,5]{0,1:T(8,128)(4,1)} %constant.99) | copy-start | bytes 124
  8.3 9.8 %collective-permute-start = (bf16[1,1,4,64,128]{4,0,3,2,1:T(2,128)(2,1)S(1)}, bf16[1,1,4,64,128]{4,0,3,2,1:T(2,128)(2,1)S(1)}, u32[]{:S(2)}, u32[]{:S(2)}) collective-permute-start(bf16[1,1,4,64,128]{4,0,3,2,1:T(2,128)(2,1)S(1)} %copy.683), channel_id=1, source_target_pairs={{0,1},{1,2},{2,3},{3,4},{4,5},{5,6},{6,7},{7,8},{8,9},{9,10},{10,1... | collective-permute-start | bytes 196616 | tf_op jit(solution)/shard_map/ppermute | solution.py:15
  20.1 150.2 %copy-start.50 = (f32[256]{0:T(256)S(1)}, f32[256]{0:T(256)}, u32[]{:S(2)}) copy-start(f32[256]{0:T(256)} %param.12) | copy-start | bytes 3076
  20.1 150.2 %copy-start.53 = (f32[256]{0:T(256)S(1)}, f32[256]{0:T(256)}, u32[]{:S(2)}) copy-start(f32[256]{0:T(256)} %param.13) | copy-start | bytes 3076
  20.5 159.5 %copy-start.47 = (bf16[3,3,3,8,4]{3,4,2,1,0:T(4,128)(2,1)S(1)}, bf16[3,3,3,8,4]{3,4,2,1,0:T(4,128)(2,1)}, u32[]{:S(2)}) copy-start(bf16[3,3,3,8,4]{3,4,2,1,0:T(4,128)(2,1)} %param.14) | copy-start | bytes 5188
  20.5 160.2 %copy-start.56 = (u32[256]{0:T(256)S(1)}, u32[256]{0:T(256)}, u32[]{:S(2)}) copy-start(u32[256]{0:T(256)} %constant.108) | copy-start | bytes 3076
  172.0 16.9 %all-to-all-start = ((bf16[64,2,256]{2,1,0:T(2,128)(2,1)}), bf16[64,2,256]{2,1,0:T(2,128)(2,1)S(1)}, u32[]{:S(2)}, u32[]{:S(2)}) async-start(bf16[64,2,256]{2,1,0:T(2,128)(2,1)} %reshape.364), calls=%async_computation | async-start | bytes 131072 | tf_op jit(solution)/shard_map/all_to_all | solution.py:86
  197.9 25.7 %copy-start.52 = (f32[4]{0:T(128)S(1)}, f32[4]{0:T(128)}, u32[]{:S(2)}) copy-start(f32[4]{0:T(128)} %param.15) | copy-start | bytes 52
  197.9 25.7 %copy-start.54 = (f32[4]{0:T(128)S(1)}, f32[4]{0:T(128)}, u32[]{:S(2)}) copy-start(f32[4]{0:T(128)} %param.16) | copy-start | bytes 52
  197.9 26.5 %copy-start.6 = (bf16[1,4,64,2,32]{2,4,3,1,0:T(8,128)(2,1)S(1)}, bf16[1,4,64,2,32]{2,4,3,1,0:T(8,128)(2,1)}, u32[]{:S(2)}) copy-start(bf16[1,4,64,2,32]{2,4,3,1,0:T(8,128)(2,1)} %param.17) | copy-start | bytes 98308
  199.6 35.7 %copy-start.48 = (bf16[3,3,3,8,4]{3,4,2,1,0:T(4,128)(2,1)S(1)}, bf16[3,3,3,8,4]{3,4,2,1,0:T(4,128)(2,1)}, u32[]{:S(2)}) copy-start(bf16[3,3,3,8,4]{3,4,2,1,0:T(4,128)(2,1)} %rev.3) | copy-start | bytes 5188
  310.0 13.3 %copy-start.10 = (f32[1,2,1,40,8]{3,4,1,2,0:T(8,128)S(1)}, f32[1,2,1,40,8]{3,4,1,2,0:T(8,128)}, u32[]{:S(2)}) copy-start(f32[1,2,1,40,8]{3,4,1,2,0:T(8,128)} %reshape.165) | copy-start | bytes 7684
  310.0 13.3 %copy-start.8 = (f32[1,2,1,40,8]{3,4,1,2,0:T(8,128)S(1)}, f32[1,2,1,40,8]{3,4,1,2,0:T(8,128)}, u32[]{:S(2)}) copy-start(f32[1,2,1,40,8]{3,4,1,2,0:T(8,128)} %reshape.167) | copy-start | bytes 7684
  310.0 16.6 %copy-start.11 = (f32[1,2,1,40,8]{3,4,1,2,0:T(8,128)S(1)}, f32[1,2,1,40,8]{3,4,1,2,0:T(8,128)}, u32[]{:S(2)}) copy-start(f32[1,2,1,40,8]{3,4,1,2,0:T(8,128)} %reshape.231) | copy-start | bytes 7684
  310.0 16.6 %copy-start.9 = (f32[1,2,1,40,8]{3,4,1,2,0:T(8,128)S(1)}, f32[1,2,1,40,8]{3,4,1,2,0:T(8,128)}, u32[]{:S(2)}) copy-start(f32[1,2,1,40,8]{3,4,1,2,0:T(8,128)} %reshape.233) | copy-start | bytes 7684
  310.7 15.9 %copy-start.7 = (f32[1,2,1,40,8]{3,4,1,2,0:T(8,128)S(1)}, f32[1,2,1,40,8]{3,4,1,2,0:T(8,128)}, u32[]{:S(2)}) copy-start(f32[1,2,1,40,8]{3,4,1,2,0:T(8,128)} %reshape.235) | copy-start | bytes 7684
  310.8 12.4 %copy-start.14 = (f32[1,2,1,40,8]{3,4,1,2,0:T(8,128)S(1)}, f32[1,2,1,40,8]{3,4,1,2,0:T(8,128)}, u32[]{:S(2)}) copy-start(f32[1,2,1,40,8]{3,4,1,2,0:T(8,128)} %reshape.161) | copy-start | bytes 7684
  310.8 12.4 %copy-start.12 = (f32[1,2,1,40,8]{3,4,1,2,0:T(8,128)S(1)}, f32[1,2,1,40,8]{3,4,1,2,0:T(8,128)}, u32[]{:S(2)}) copy-start(f32[1,2,1,40,8]{3,4,1,2,0:T(8,128)} %reshape.163) | copy-start | bytes 7684
  310.8 15.4 %copy-start.16 = (f32[1,2,1,40,8]{3,4,1,2,0:T(8,128)S(1)}, f32[1,2,1,40,8]{3,4,1,2,0:T(8,128)}, u32[]{:S(2)}) copy-start(f32[1,2,1,40,8]{3,4,1,2,0:T(8,128)} %reshape.205) | copy-start | bytes 7684
  310.8 15.7 %copy-start.15 = (f32[1,2,1,40,8]{3,4,1,2,0:T(8,128)S(1)}, f32[1,2,1,40,8]{3,4,1,2,0:T(8,128)}, u32[]{:S(2)}) copy-start(f32[1,2,1,40,8]{3,4,1,2,0:T(8,128)} %reshape.227) | copy-start | bytes 7684
  310.8 15.7 %copy-start.13 = (f32[1,2,1,40,8]{3,4,1,2,0:T(8,128)S(1)}, f32[1,2,1,40,8]{3,4,1,2,0:T(8,128)}, u32[]{:S(2)}) copy-start(f32[1,2,1,40,8]{3,4,1,2,0:T(8,128)} %reshape.229) | copy-start | bytes 7684
  311.7 11.5 %copy-start.21 = (f32[1,2,1,40,8]{3,4,1,2,0:T(8,128)S(1)}, f32[1,2,1,40,8]{3,4,1,2,0:T(8,128)}, u32[]{:S(2)}) copy-start(f32[1,2,1,40,8]{3,4,1,2,0:T(8,128)} %reshape.157) | copy-start | bytes 7684
  311.7 11.5 %copy-start.18 = (f32[1,2,1,40,8]{3,4,1,2,0:T(8,128)S(1)}, f32[1,2,1,40,8]{3,4,1,2,0:T(8,128)}, u32[]{:S(2)}) copy-start(f32[1,2,1,40,8]{3,4,1,2,0:T(8,128)} %reshape.159) | copy-start | bytes 7684
  311.7 14.8 %copy-start.19 = (f32[1,2,1,40,8]{3,4,1,2,0:T(8,128)S(1)}, f32[1,2,1,40,8]{3,4,1,2,0:T(8,128)}, u32[]{:S(2)}) copy-start(f32[1,2,1,40,8]{3,4,1,2,0:T(8,128)} %reshape.225) | copy-start | bytes 7684
  312.6 10.6 %copy-start.24 = (f32[1,2,1,40,8]{3,4,1,2,0:T(8,128)S(1)}, f32[1,2,1,40,8]{3,4,1,2,0:T(8,128)}, u32[]{:S(2)}) copy-start(f32[1,2,1,40,8]{3,4,1,2,0:T(8,128)} %reshape.155) | copy-start | bytes 7684
  312.6 13.9 %copy-start.25 = (f32[1,2,1,40,8]{3,4,1,2,0:T(8,128)S(1)}, f32[1,2,1,40,8]{3,4,1,2,0:T(8,128)}, u32[]{:S(2)}) copy-start(f32[1,2,1,40,8]{3,4,1,2,0:T(8,128)} %reshape.221) | copy-start | bytes 7684
  312.6 13.9 %copy-start.22 = (f32[1,2,1,40,8]{3,4,1,2,0:T(8,128)S(1)}, f32[1,2,1,40,8]{3,4,1,2,0:T(8,128)}, u32[]{:S(2)}) copy-start(f32[1,2,1,40,8]{3,4,1,2,0:T(8,128)} %reshape.223) | copy-start | bytes 7684
  313.5 9.7 %copy-start.30 = (f32[1,2,1,40,8]{3,4,1,2,0:T(8,128)S(1)}, f32[1,2,1,40,8]{3,4,1,2,0:T(8,128)}, u32[]{:S(2)}) copy-start(f32[1,2,1,40,8]{3,4,1,2,0:T(8,128)} %reshape.151) | copy-start | bytes 7684
  313.5 9.7 %copy-start.27 = (f32[1,2,1,40,8]{3,4,1,2,0:T(8,128)S(1)}, f32[1,2,1,40,8]{3,4,1,2,0:T(8,128)}, u32[]{:S(2)}) copy-start(f32[1,2,1,40,8]{3,4,1,2,0:T(8,128)} %reshape.153) | copy-start | bytes 7684
  313.5 12.9 %copy-start.31 = (f32[1,2,1,40,8]{3,4,1,2,0:T(8,128)S(1)}, f32[1,2,1,40,8]{3,4,1,2,0:T(8,128)}, u32[]{:S(2)}) copy-start(f32[1,2,1,40,8]{3,4,1,2,0:T(8,128)} %reshape.217) | copy-start | bytes 7684
  313.5 12.9 %copy-start.28 = (f32[1,2,1,40,8]{3,4,1,2,0:T(8,128)S(1)}, f32[1,2,1,40,8]{3,4,1,2,0:T(8,128)}, u32[]{:S(2)}) copy-start(f32[1,2,1,40,8]{3,4,1,2,0:T(8,128)} %reshape.219) | copy-start | bytes 7684
  314.3 8.7 %copy-start.35 = (f32[1,2,1,40,8]{3,4,1,2,0:T(8,128)S(1)}, f32[1,2,1,40,8]{3,4,1,2,0:T(8,128)}, u32[]{:S(2)}) copy-start(f32[1,2,1,40,8]{3,4,1,2,0:T(8,128)} %reshape.147) | copy-start | bytes 7684
  314.3 8.8 %copy-start.33 = (f32[1,2,1,40,8]{3,4,1,2,0:T(8,128)S(1)}, f32[1,2,1,40,8]{3,4,1,2,0:T(8,128)}, u32[]{:S(2)}) copy-start(f32[1,2,1,40,8]{3,4,1,2,0:T(8,128)} %reshape.149) | copy-start | bytes 7684
  314.3 12.0 %copy-start.36 = (f32[1,2,1,40,8]{3,4,1,2,0:T(8,128)S(1)}, f32[1,2,1,40,8]{3,4,1,2,0:T(8,128)}, u32[]{:S(2)}) copy-start(f32[1,2,1,40,8]{3,4,1,2,0:T(8,128)} %reshape.213) | copy-start | bytes 7684
  314.4 12.0 %copy-start.34 = (f32[1,2,1,40,8]{3,4,1,2,0:T(8,128)S(1)}, f32[1,2,1,40,8]{3,4,1,2,0:T(8,128)}, u32[]{:S(2)}) copy-start(f32[1,2,1,40,8]{3,4,1,2,0:T(8,128)} %reshape.215) | copy-start | bytes 7684
  315.2 7.8 %copy-start.39 = (f32[1,2,1,40,8]{3,4,1,2,0:T(8,128)S(1)}, f32[1,2,1,40,8]{3,4,1,2,0:T(8,128)}, u32[]{:S(2)}) copy-start(f32[1,2,1,40,8]{3,4,1,2,0:T(8,128)} %reshape.143) | copy-start | bytes 7684
  315.2 7.8 %copy-start.37 = (f32[1,2,1,40,8]{3,4,1,2,0:T(8,128)S(1)}, f32[1,2,1,40,8]{3,4,1,2,0:T(8,128)}, u32[]{:S(2)}) copy-start(f32[1,2,1,40,8]{3,4,1,2,0:T(8,128)} %reshape.145) | copy-start | bytes 7684
  315.2 11.1 %copy-start.40 = (f32[1,2,1,40,8]{3,4,1,2,0:T(8,128)S(1)}, f32[1,2,1,40,8]{3,4,1,2,0:T(8,128)}, u32[]{:S(2)}) copy-start(f32[1,2,1,40,8]{3,4,1,2,0:T(8,128)} %reshape.209) | copy-start | bytes 7684
  315.2 11.1 %copy-start.38 = (f32[1,2,1,40,8]{3,4,1,2,0:T(8,128)S(1)}, f32[1,2,1,40,8]{3,4,1,2,0:T(8,128)}, u32[]{:S(2)}) copy-start(f32[1,2,1,40,8]{3,4,1,2,0:T(8,128)} %reshape.211) | copy-start | bytes 7684
  316.1 10.1 %copy-start.46 = (f32[1,2,1,40,8]{3,4,1,2,0:T(8,128)S(1)}, f32[1,2,1,40,8]{3,4,1,2,0:T(8,128)}, u32[]{:S(2)}) copy-start(f32[1,2,1,40,8]{3,4,1,2,0:T(8,128)} %reshape.197) | copy-start | bytes 7684
  316.1 10.1 %copy-start.45 = (f32[1,2,1,40,8]{3,4,1,2,0:T(8,128)S(1)}, f32[1,2,1,40,8]{3,4,1,2,0:T(8,128)}, u32[]{:S(2)}) copy-start(f32[1,2,1,40,8]{3,4,1,2,0:T(8,128)} %reshape.199) | copy-start | bytes 7684
  316.1 10.1 %copy-start.44 = (f32[1,2,1,40,8]{3,4,1,2,0:T(8,128)S(1)}, f32[1,2,1,40,8]{3,4,1,2,0:T(8,128)}, u32[]{:S(2)}) copy-start(f32[1,2,1,40,8]{3,4,1,2,0:T(8,128)} %reshape.201) | copy-start | bytes 7684
  316.1 10.1 %copy-start.43 = (f32[1,2,1,40,8]{3,4,1,2,0:T(8,128)S(1)}, f32[1,2,1,40,8]{3,4,1,2,0:T(8,128)}, u32[]{:S(2)}) copy-start(f32[1,2,1,40,8]{3,4,1,2,0:T(8,128)} %reshape.203) | copy-start | bytes 7684
  316.1 10.2 %copy-start.42 = (f32[1,2,1,40,8]{3,4,1,2,0:T(8,128)S(1)}, f32[1,2,1,40,8]{3,4,1,2,0:T(8,128)}, u32[]{:S(2)}) copy-start(f32[1,2,1,40,8]{3,4,1,2,0:T(8,128)} %reshape.207) | copy-start | bytes 7684
  339.2 14.9 %all-to-all-start.1 = ((f32[64,1,512]{2,1,0:T(1,128)}), f32[64,1,512]{2,1,0:T(1,128)S(1)}, u32[]{:S(2)}, u32[]{:S(2)}) async-start(f32[64,1,512]{2,1,0:T(1,128)} %reshape.366), calls=%async_computation.1 | async-start | bytes 262144 | tf_op jit(solution)/shard_map/all_to_all | solution.py:145
  344.7 281.9 %all-reduce.10.cloned.1.call-start = ((), (), s32[]{:S(2)}) async-start(), calls=%async_computation.2 | async-start | bytes 7077888
  356.2 77.5 %copy-start.2 = (bf16[1,3,4,64,128]{4,0,3,2,1:T(2,128)(2,1)S(1)}, bf16[1,3,4,64,128]{4,0,3,2,1:T(2,128)(2,1)}, u32[]{:S(2)}) copy-start(bf16[1,3,4,64,128]{4,0,3,2,1:T(2,128)(2,1)} %copy-done.1) | copy-start | bytes 589828
  (13 other events, 58.2 us)
Sparse Core Ops, SparseCore 0:
  436.7 189.8 all-reduce.9
